TPU v7x, 32 devices: a whole 2x2x4 slice. The times are simulated.
32 devices in a mesh: tm: 8 (over z, y), rows: 4 (over x, core).
Axes of the slice: x: 2, y: 2, z: 4, core: 2. Of those that a mesh axis runs over, the one named last changes fastest.
Arguments:
- phases: bfloat16 [16, 512, 512], P('tm', 'rows'), may hold values from -6 to 6
- focal_data: bfloat16 [16, 2, 256, 256], P('tm', None, 'rows'), may hold values from -6 to 6
- shifts: int32 [16, 2], P('tm'), may hold values from 0 to 2, as said below
- pupil_mask: int32 [512, 512], P('rows'), may hold values 0 or 1
Outputs:
- adjoint_field: float32 [16, 512, 512], P('tm', 'rows')
- wind_grad: float32 [2], replicated
Inputs may be any that keep to these rules, and one draw needn't show every extreme that they name: `shifts`: column 0 is a frame's shift along pupil rows, 0 or 1, and sums over all frames to exactly 8; column 1 is its shift along pupil columns, 0 to 2.
All inputs are finite; a program needn't handle non-finite values. No bound on the sum of `pupil_mask` on one device may be relied on, other than what follows from the above.
Results may differ from a plain program's by a relative error of at most 0.0054.
Values may be sent and summed in bfloat16 or wider, within the bound.
No kernel may reach another device: no remote copies, remote signals or barrier semaphores. Data moves between devices by JAX's collectives and lax.ppermute only.
A program may use at most 128 MiB of HBM per device.

v0:
```python
import math
import jax
import jax.numpy as jnp
from jax import lax
from jax.sharding import PartitionSpec as P

PUPIL = 512
FOCAL = 256
decay_rate = 0.999


def from_behind(value, axis, steps):
    count = lax.axis_size(axis)
    first, last = (max(0, -steps), min(count, count - steps))
    return lax.ppermute(value, axis, [(source, source + steps) for source in range(first, last)])


def carried_in(part, axis, combine, identity):
    count = lax.axis_size(axis)
    place = lax.axis_index(axis)
    ahead = count - 1 - place
    gathered = jax.tree.map(lambda a: lax.all_gather(a, axis), part)
    state = jax.tree.map(lambda a, e: jnp.zeros_like(a) + jnp.asarray(e, a.dtype), part, identity)

    def one(step, state):
        source = count - 1 - step
        return combine(
            state, jax.tree.map(lambda a: lax.dynamic_index_in_dim(a, source, 0, False), gathered)
        )

    return lax.fori_loop(0, ahead, one, state)


def tables(row_total):
    focal_pos = jnp.arange(FOCAL, dtype=jnp.int32) - FOCAL // 2
    pupil_pos = jnp.arange(row_total, dtype=jnp.int32) - PUPIL // 2
    turns = jnp.mod(focal_pos[:, None] * pupil_pos[None, :], 2 * PUPIL)
    angle = turns.astype(jnp.float32) * (math.pi / PUPIL)
    factor = 1.0 / math.sqrt(PUPIL)
    return (
        (jnp.cos(angle) * factor).astype(jnp.bfloat16),
        (-jnp.sin(angle) * factor).astype(jnp.bfloat16),
    )


def shift_back(field_in, shift_rows, shift_cols, pad_rows):
    cols_total = field_in.shape[1]
    padded = jnp.pad(field_in, ((0, pad_rows), (0, 0)))
    start_row = jnp.minimum(shift_rows, pad_rows).astype(jnp.int32)
    moved = lax.dynamic_slice(padded, (start_row, jnp.zeros((), jnp.int32)), field_in.shape)
    start_col = jnp.minimum(shift_cols, cols_total).astype(jnp.int32)
    rolled = jnp.roll(moved, -start_col, axis=1)
    keep = jnp.arange(cols_total, dtype=jnp.int32) < cols_total - start_col
    return jnp.where(keep[None, :], rolled, jnp.zeros_like(rolled))


def adjoint_rows(cos_part, sin_part, resid, cos_full, sin_full, live):
    real_part = resid[:, 0]
    imag_part = resid[:, 1]
    w_real = (
        jnp.einsum("qn,kqs->kns", cos_part, real_part, preferred_element_type=jnp.float32)
        + jnp.einsum("qn,kqs->kns", sin_part, imag_part, preferred_element_type=jnp.float32)
    ).astype(jnp.bfloat16)
    w_imag = (
        jnp.einsum("qn,kqs->kns", cos_part, imag_part, preferred_element_type=jnp.float32)
        - jnp.einsum("qn,kqs->kns", sin_part, real_part, preferred_element_type=jnp.float32)
    ).astype(jnp.bfloat16)
    summed = jnp.einsum(
        "kns,sp->knp", w_real, cos_full, preferred_element_type=jnp.float32
    ) + jnp.einsum("kns,sp->knp", w_imag, sin_full, preferred_element_type=jnp.float32)
    return jnp.where(live[None], summed, jnp.zeros_like(summed))


def on_device(phases, focal_data, shifts, pupil_mask):
    frame_count = phases.shape[0]
    block = phases.shape[1]
    width = phases.shape[2]
    halo_rows = width // (4 * lax.axis_size("rows"))
    window = block + halo_rows
    frames_all = frame_count * lax.axis_size("tm")
    row_start = lax.axis_index("rows") * block
    cos_t, sin_t = tables(width)
    cos_rows = lax.dynamic_slice_in_dim(cos_t, row_start, block, 1)
    sin_rows = lax.dynamic_slice_in_dim(sin_t, row_start, block, 1)
    live = pupil_mask == 1
    masked = jnp.where(live[None], phases, jnp.zeros_like(phases))
    y_real = jnp.einsum("kbp,qp->kbq", masked, cos_t, preferred_element_type=jnp.float32).astype(
        jnp.bfloat16
    )
    y_imag = jnp.einsum("kbp,qp->kbq", masked, sin_t, preferred_element_type=jnp.float32).astype(
        jnp.bfloat16
    )
    e_real = jnp.einsum(
        "qb,kbs->kqs", cos_rows, y_real, preferred_element_type=jnp.float32
    ) - jnp.einsum("qb,kbs->kqs", sin_rows, y_imag, preferred_element_type=jnp.float32)
    e_imag = jnp.einsum(
        "qb,kbs->kqs", cos_rows, y_imag, preferred_element_type=jnp.float32
    ) + jnp.einsum("qb,kbs->kqs", sin_rows, y_real, preferred_element_type=jnp.float32)
    partial_field = jnp.stack([e_real, e_imag], axis=1)
    placed = lax.dynamic_update_slice_in_dim(
        jnp.zeros_like(partial_field),
        focal_data.astype(jnp.float32),
        lax.axis_index("rows") * focal_data.shape[2],
        2,
    )
    total = lax.psum(partial_field - placed, "rows")
    resid = (-total).astype(jnp.bfloat16)
    grad = adjoint_rows(cos_rows, sin_rows, resid, cos_t, sin_t, live)
    outgoing = jnp.concatenate([grad[:, :halo_rows], phases[:, :1].astype(jnp.float32)], axis=1)
    incoming = from_behind(outgoing, "rows", -1)
    grad_window = jnp.concatenate([grad, incoming[:, :halo_rows]], axis=1)
    next_phase = incoming[:, halo_rows]
    lam_next = jnp.zeros((window, width), jnp.float32)
    local_lams = [lam_next] * frame_count
    for frame in reversed(range(frame_count)):
        lam_next = grad_window[frame] + decay_rate * shift_back(
            lam_next, shifts[frame, 0], shifts[frame, 1], halo_rows
        )
        local_lams[frame] = lam_next

    def compose(earlier, later):
        field_late, rows_late, cols_late = earlier
        field_early, rows_early, cols_early = later
        moved = shift_back(field_late, rows_early, cols_early, halo_rows)
        return (field_early + moved, rows_early + rows_late, cols_early + cols_late)

    time_index = lax.axis_index("tm").astype(jnp.float32)
    frames_float = jnp.float32(frame_count)
    start_weight = jnp.power(jnp.float32(decay_rate), time_index * frames_float)
    after_weight = jnp.power(jnp.float32(decay_rate), (time_index + 1.0) * frames_float)
    segment = (start_weight * local_lams[0], jnp.sum(shifts[:, 0]), jnp.sum(shifts[:, 1]))
    identity = (
        jnp.zeros((window, width), jnp.float32),
        jnp.zeros((), jnp.int32),
        jnp.zeros((), jnp.int32),
    )
    carried = carried_in(segment, "tm", compose, identity)
    carry_field = carried[0] / after_weight
    cum_rows = jnp.zeros((), jnp.int32)
    cum_cols = jnp.zeros((), jnp.int32)
    factor_now = 1.0
    results = [None] * frame_count
    wind_terms = jnp.zeros((2,), jnp.float32)
    for frame in reversed(range(frame_count)):
        cum_rows = cum_rows + shifts[frame, 0]
        cum_cols = cum_cols + shifts[frame, 1]
        factor_now = factor_now * decay_rate
        lam_now = (
            local_lams[frame][:block]
            + factor_now * shift_back(carry_field, cum_rows, cum_cols, halo_rows)[:block]
        )
        results[frame] = lam_now
        prior = lam_now - grad[frame]
        phase_wide = phases[frame].astype(jnp.float32)
        down_diff = jnp.concatenate([phase_wide[1:], next_phase[frame][None]], axis=0) - phase_wide
        side_diff = (
            jnp.concatenate([phase_wide[:, 1:], jnp.zeros((block, 1), jnp.float32)], axis=1)
            - phase_wide
        )
        wind_terms = wind_terms + jnp.stack(
            [jnp.sum(prior * down_diff), jnp.sum(prior * side_diff)]
        )
    wind_total = lax.psum(wind_terms, ("tm", "rows"))
    wind_grad = -wind_total / (width * frames_all)
    return (jnp.stack(results), wind_grad)


def solution(mesh):
    in_specs = (P("tm", "rows", None), P("tm", None, "rows", None), P("tm", None), P("rows", None))
    out_specs = (P("tm", "rows", None), P())
    return jax.shard_map(
        on_device, mesh=mesh, in_specs=in_specs, out_specs=out_specs, check_vma=False
    )
```

profile of v0, /device:TPU:10, one launch (start us, length us, event | category | flops | bytes accessed | tf_op | source)
XLA Modules:
  0.0 205.0 jit_solution(5280239042535664271)
XLA Ops:
  7.2 0.0 copy-start
  7.2 0.0 all-reduce.11.cloned.1.call-start
  7.2 1.0 broadcast_compare_fusion
  8.2 2.5 %multiply_convert_fusion = (bf16[256,512]{1,0:T(8,128)(2,1)S(1)}, bf16[256,512]{1,0:T(8,128)(2,1)S(1)}) fusion(s32[512]{0:T(512)S(1)} %iota_add_fusion, s32[256]{0:T(256)S(1)} %iota_add_fusion.1), kind=kLoop, calls=%fused_computation.43 | loop fusion | flops 2490368 | bytes 527360 | tf_op jit(solution)/shard_map/convert_element_type | solution.py:42
  10.7 0.0 copy-start.1
  10.7 3.3 %convolution_convert_fusion = bf16[2,128,256]{2,1,0:T(8,128)(2,1)S(1)} fusion(bf16[2,128,512]{2,1,0:T(8,128)(2,1)} %param.8, pred[128,512]{1,0:T(8,128)(4,1)S(1)} %broadcast_compare_fusion, s32[512]{0:T(512)S(1)} %iota_add_fusion, s32[256]{0:T(256)S(1)} %iota_add_fusion.1), kind=kOutput, calls=%fused_computation.17 | convolution fusion | flops 69533696 | bytes 461824 | tf_op jit(solution)/shard_map/kbp,qp->kbq/dot_general | solution.py:90
  14.0 2.2 %convolution_convert_fusion.1 = bf16[2,128,256]{2,1,0:T(8,128)(2,1)S(1)} fusion(bf16[2,128,512]{2,1,0:T(8,128)(2,1)S(1)} %copy-done, pred[128,512]{1,0:T(8,128)(4,1)S(1)} %broadcast_compare_fusion, s32[512]{0:T(512)S(1)} %iota_add_fusion, s32[256]{0:T(256)S(1)} %iota_add_fusion.1), kind=kOutput, calls=%fused_computation.18 | convolution fusion | flops 69402624 | bytes 461824 | tf_op jit(solution)/shard_map/kbp,qp->kbq/dot_general | solution.py:87
  16.2 0.0 copy-start.2
  16.2 0.2 fusion.55
  16.5 0.2 fusion.57
  16.7 0.3 fusion.3
  17.0 0.3 fusion.4
  17.3 0.1 copy.15
  17.4 0.1 broadcast_in_dim.73
  17.5 0.0 copy-start.3
  17.5 1.4 dynamic_update_slice.3
  18.9 1.2 maximum_subtract_fusion
  20.1 0.0 all-reduce.11.cloned.1.call-update
  20.1 0.0 all-gather.3.cloned.1.call-start
  20.1 0.6 fusion.104
  23.2 34.5 %all-reduce.11.cloned.1.call-done = f32[2,2,256,256]{2,3,0,1:T(8,128)} async-done(((f32[2,2,256,256]{2,3,0,1:T(8,128)}), f32[2,2,256,256]{2,3,0,1:T(8,128)}) %all-reduce.11.cloned.1.call-update) | async-done | bytes 1048592 | tf_op jit(solution)/shard_map/psum | solution.py:106
  57.7 1.3 negate_convert_fusion
  59.0 0.2 fusion.43
  59.3 0.2 fusion.44
  59.5 2.2 %fusion.10 = f32[2,128,512]{2,1,0:T(8,128)S(1)} fusion(f32[2,256,128]{1,2,0:T(8,128)S(1)} %fusion.43, bf16[2,2,256,256]{2,3,0,1:T(8,128)(2,1)S(1)} %negate_convert_fusion, s32[512]{0:T(512)S(1)} %iota_add_fusion, s32[256]{0:T(256)S(1)} %iota_add_fusion.1, bf16[256,512]{1,0:T(8,128)(2,1)S(1)} %get-tuple-element.162, s32[]{:T(128)S(6)} %select_n.122), kind=kOutput, calls=%fused_computation.21 | convolution fusion | flops 102891520 | bytes 1117188 | tf_op jit(solution)/shard_map/kns,sp->knp/dot_general | solution.py:68
  61.7 3.1 %fusion.5 = f32[2,128,512]{2,1,0:T(8,128)S(1)} fusion(f32[2,128,512]{2,1,0:T(8,128)S(1)} %fusion.10, f32[2,256,128]{1,2,0:T(8,128)S(1)} %fusion.44, pred[128,512]{1,0:T(8,128)(4,1)S(1)} %broadcast_compare_fusion, bf16[2,2,256,256]{2,3,0,1:T(8,128)(2,1)S(1)} %negate_convert_fusion, s32[512]{0:T(512)S(1)} %iota_add_fusion, s32[256]{0:T(256)S(1)} %iota_add_fusion.1, ...), kind=kOutput, calls=%fused_computation.12 | convolution fusion | flops 103284736 | bytes 1707012 | tf_op jit(solution)/shard_map/kns,sp->knp/dot_general | solution.py:70
  64.8 2.1 %collective-permute-start = (f32[2,33,512]{2,1,0:T(8,128)S(1)}, f32[2,33,512]{2,1,0:T(8,128)S(1)}, u32[]{:S(2)}, u32[]{:S(2)}) collective-permute-start(f32[2,33,512]{2,1,0:T(8,128)S(1)} %pad_maximum_fusion.2), channel_id=1, source_target_pairs={{1,0},{2,1},{3,2},{5,4},{6,5},{7,6},{9,8},{10,9},{11,10},{13,12},{... | collective-permute-start | bytes 405512 | tf_op jit(solution)/shard_map/ppermute | solution.py:15
  67.0 0.0 copy-start.4
  68.4 1.2 collective-permute-done
  69.6 0.2 fusion.21
  69.9 1.0 broadcast_multiply_fusion
  70.9 0.0 all-gather.3.cloned.1.call-update
  70.9 0.6 dynamic-slice
  71.5 0.8 slice_reduce_fusion
  72.3 1.4 dynamic-update-slice
  73.6 1.3 dynamic-update-slice.1
  75.0 10.4 %all-reduce.8 = (s32[8]{0:T(128)S(1)}, s32[8]{0:T(128)S(1)}) all-reduce(s32[8]{0:T(128)S(1)} %dynamic-update-slice, s32[8]{0:T(128)S(1)} %dynamic-update-slice.1), channel_id=1, replica_groups=mesh['tm'=8,'rows'=4] {'tm'}, use_global_device_ids=true, to_apply=%add.6 | all-reduce | flops 16 | bytes 128
  86.7 0.1 slice_convert_fusion.1
  86.8 0.1 slice.142
  87.0 0.1 slice.146
  87.1 0.1 slice_bitcast_fusion
  87.2 39.7 %all-gather.3.cloned.1.call-done = f32[1280,512]{1,0:T(8,128)} async-done(((f32[160,512]{1,0:T(8,128)}), f32[1280,512]{1,0:T(8,128)}) %all-gather.3.cloned.1.call-update) | async-done | bytes 2621456 | tf_op jit(solution)/shard_map/all_gather | solution.py:22
  126.9 19.4 %while.16 = (s32[]{:T(128)}, f32[160,512]{1,0:T(8,128)S(1)}, s32[]{:T(128)}, f32[8,160,512]{2,1,0:T(8,128)}, s32[8]{0:T(128)S(1)}, /*index=5*/s32[8]{0:T(128)S(1...) while((s32[]{:T(128)}, f32[160,512]{1,0:T(8,128)S(1)}, ...), condition=%wide.region_4.6_spmd, body=%wide.region_3.5_spmd.sunk | while | flops 246299 | bytes 1639884 | solution.py:31
  126.9 0.6 dynamic_slice.173
  128.1 0.7 dynamic_slice.174
  129.5 1.2 fusion.110
  130.8 0.6 dynamic_slice.173
  132.0 0.7 dynamic_slice.174
  133.4 1.2 fusion.110
  134.6 0.6 dynamic_slice.173
  135.9 0.7 dynamic_slice.174
  137.3 1.2 fusion.110
  138.5 0.6 dynamic_slice.173
  139.8 0.7 dynamic_slice.174
  141.1 1.2 fusion.110
  142.4 0.6 dynamic_slice.173
  143.7 0.7 dynamic_slice.174
  145.0 1.2 fusion.110
  146.3 0.1 pad_dynamic-slice_fusion.11
  146.4 1.1 fusion.38
  147.5 2.6 %maximum_add_fusion = f32[2]{0:T(128)S(1)} fusion(f32[1]{0:T(128)} %bitcast.37, f32[1]{0:T(128)} %bitcast.36, f32[1]{0:T(128)} %bitcast.43, f32[1]{0:T(128)} %bitcast.42), kind=kLoop, calls=%fused_computation.140 | loop fusion | flops 6 | bytes 24 | tf_op jit(solution)/shard_map/add | solution.py:160
  150.1 46.7 %psum.15 = f32[2]{0:T(128)S(1)} all-reduce(f32[2]{0:T(128)S(1)} %maximum_add_fusion), channel_id=1, replica_groups=mesh['tm'=8,'rows'=4] {'tm','rows'}, use_global_device_ids=true, to_apply=%region_9.11 | all-reduce | flops 2 | bytes 16 | tf_op jit(solution)/shard_map/psum | solution.py:163
  196.9 0.5 negate_multiply_fusion
  197.4 0.8 pad_maximum_fusion
  (30 shorter events, 0.4 us)
Async XLA Ops:
  7.2 6.8 %copy-start = (bf16[2,128,512]{2,1,0:T(8,128)(2,1)S(1)}, bf16[2,128,512]{2,1,0:T(8,128)(2,1)}, u32[]{:S(2)}) copy-start(bf16[2,128,512]{2,1,0:T(8,128)(2,1)} %param.8) | copy-start | bytes 786436
  7.2 50.5 %all-reduce.11.cloned.1.call-start = ((), (), s32[]{:S(2)}) async-start(), calls=%async_computation | async-start | bytes 2097152 | tf_op jit(solution)/shard_map/psum | solution.py:106
  10.7 48.8 %copy-start.1 = (bf16[256,512]{1,0:T(8,128)(2,1)}, bf16[256,512]{1,0:T(8,128)(2,1)S(1)}, u32[]{:S(2)}) copy-start(bf16[256,512]{1,0:T(8,128)(2,1)S(1)} %get-tuple-element.162) | copy-start | bytes 786436
  16.2 1.1 copy-start.2
  17.5 2.6 %copy-start.3 = (s32[2,2]{1,0:T(2,128)S(1)}, s32[2,2]{1,0:T(2,128)}, u32[]{:S(2)}) copy-start(s32[2,2]{1,0:T(2,128)} %param.10) | copy-start | bytes 52
  20.1 106.8 %all-gather.3.cloned.1.call-start = ((), (), s32[]{:S(2)}) async-start(), calls=%async_computation.1 | async-start | bytes 2949120 | tf_op jit(solution)/shard_map/all_gather | solution.py:22
  64.8 4.7 %collective-permute-start = (f32[2,33,512]{2,1,0:T(8,128)S(1)}, f32[2,33,512]{2,1,0:T(8,128)S(1)}, u32[]{:S(2)}, u32[]{:S(2)}) collective-permute-start(f32[2,33,512]{2,1,0:T(8,128)S(1)} %pad_maximum_fusion.2), channel_id=1, source_target_pairs={{1,0},{2,1},{3,2},{5,4},{6,5},{7,6},{9,8},{10,9},{11,10},{13,12},{... | collective-permute-start | bytes 405512 | tf_op jit(solution)/shard_map/ppermute | solution.py:15
  67.0 3.9 %copy-start.4 = (u32[32]{0:T(128)S(1)}, u32[32]{0:T(128)}, u32[]{:S(2)}) copy-start(u32[32]{0:T(128)} %constant.215) | copy-start | bytes 388
Sparse Core Ops, SparseCore 0:
  20.2 37.4 all-reduce.10
  71.0 55.8 all-gather.2
where the time goes:
time: 206 us; the launch traced here: 205 us
  waiting for transfers between devices  75.4 us (37%)
  blocking collectives  57.1 us (28%)
  between operations  19.6 us (10%)
  other arithmetic  19.3 us (9%)
  local copies, waits for them, and re-layouts  12.5 us (6%)
  matrix products  12.2 us (6%)
  loops' own time  6.83 us (3%)
  starting transfers between devices  2.18 us (1%)
    psum x1, blocking collectives, on_device(): wind_total = lax.psum(wind_terms, ('tm', 'rows'))  46.7 us
    all_gather x1, waiting for transfers between devices, carried_in(): gathered = jax.tree.map(lambda a: lax.all_gather(a, axis), part)  39.7 us
    psum x1, waiting for transfers between devices, on_device(): total = lax.psum(partial_field - placed, 'rows')  34.5 us
    unnamed x1, blocking collectives  10.4 us
    another operation x1, loops' own time, carried_in(): return lax.fori_loop(0, ahead, one, state)  6.83 us
    dynamic_slice x10, local copies, waits for them, and re-layouts, one(): lax.dynamic_index_in_dim(a, source, 0, False)  6.21 us
    add x5, other arithmetic, compose(): return (field_early + moved, rows_early + rows_late, cols_early + cols_late)  6.12 us
  transfers between devices with their start and end apart: 3, of which 3 were waited for; matrix products, arithmetic and copies ran while one was open for 3% of the time, Pallas kernels for 0%

commit v1 on v0

--- a/solution.py
+++ b/solution.py
@@ -103,7 +103,7 @@
         lax.axis_index("rows") * focal_data.shape[2],
         2,
     )
-    total = lax.psum(partial_field - placed, "rows")
+    total = jnp.sum(lax.all_gather(partial_field - placed, "rows"), axis=0)
     resid = (-total).astype(jnp.bfloat16)
     grad = adjoint_rows(cos_rows, sin_rows, resid, cos_t, sin_t, live)
     outgoing = jnp.concatenate([grad[:, :halo_rows], phases[:, :1].astype(jnp.float32)], axis=1)

time: 206 us -> 205 us (level)
  waiting for transfers between devices: 75.4 us -> 73 us
    psum x1 -> x0, waiting for transfers between devices: 34.5 us -> none  [on_device(): total = lax.psum(partial_field - placed, 'rows')]
    all_gather x0 -> x1, waiting for transfers between devices: none -> 31.9 us  [on_device(): total = jnp.sum(lax.all_gather(partial_field - placed, 'rows'), axis=0)]
    reduce_sum x0 -> x1, other arithmetic: none -> 2.6 us  [on_device(): total = jnp.sum(lax.all_gather(partial_field - placed, 'rows'), axis=0)]
where the time goes in v1:
time: 205 us; the launch traced here: 204 us
  waiting for transfers between devices  73 us (36%)
  blocking collectives  56.9 us (28%)
  other arithmetic  20.6 us (10%)
  between operations  19.7 us (10%)
  matrix products  12.2 us (6%)
  local copies, waits for them, and re-layouts  12.1 us (6%)
  loops' own time  6.46 us (3%)
  starting transfers between devices  3.49 us (2%)
    psum x1, blocking collectives, on_device(): wind_total = lax.psum(wind_terms, ('tm', 'rows'))  46.4 us
    all_gather x1, waiting for transfers between devices, carried_in(): gathered = jax.tree.map(lambda a: lax.all_gather(a, axis), part)  39.8 us
    all_gather x1, waiting for transfers between devices, on_device(): total = jnp.sum(lax.all_gather(partial_field - placed, 'rows'), axis=0)  31.9 us
    unnamed x1, blocking collectives  10.4 us
    another operation x1, loops' own time, carried_in(): return lax.fori_loop(0, ahead, one, state)  6.46 us
    add x5, other arithmetic, compose(): return (field_early + moved, rows_early + rows_late, cols_early + cols_late)  6.12 us
    dynamic_slice x10, local copies, waits for them, and re-layouts, one(): lax.dynamic_index_in_dim(a, source, 0, False)  5.85 us
  transfers between devices with their start and end apart: 3, of which 3 were waited for; matrix products, arithmetic and copies ran while one was open for 3% of the time, Pallas kernels for 0%

profile of v1, /device:TPU:10, one launch (start us, length us, event | category | flops | bytes accessed | tf_op | source)
XLA Modules:
  0.0 204.4 jit_solution(16034374598653330286)
XLA Ops:
  7.2 0.0 all-gather.5.cloned.1.call-start
  7.2 1.0 broadcast_compare_fusion
  8.2 2.5 %multiply_convert_fusion = (bf16[256,512]{1,0:T(8,128)(2,1)S(1)}, bf16[256,512]{1,0:T(8,128)(2,1)S(1)}) fusion(s32[512]{0:T(512)S(1)} %iota_add_fusion, s32[256]{0:T(256)S(1)} %iota_add_fusion.1), kind=kLoop, calls=%fused_computation.43 | loop fusion | flops 2490368 | bytes 527360 | tf_op jit(solution)/shard_map/convert_element_type | solution.py:42
  10.7 0.0 copy-start.1
  10.7 3.3 %convolution_convert_fusion = bf16[2,128,256]{2,1,0:T(8,128)(2,1)S(1)} fusion(bf16[2,128,512]{2,1,0:T(8,128)(2,1)} %param.8, pred[128,512]{1,0:T(8,128)(4,1)S(1)} %broadcast_compare_fusion, s32[512]{0:T(512)S(1)} %iota_add_fusion, s32[256]{0:T(256)S(1)} %iota_add_fusion.1), kind=kOutput, calls=%fused_computation.17 | convolution fusion | flops 69533696 | bytes 461824 | tf_op jit(solution)/shard_map/kbp,qp->kbq/dot_general | solution.py:90
  14.0 2.2 %convolution_convert_fusion.1 = bf16[2,128,256]{2,1,0:T(8,128)(2,1)S(1)} fusion(bf16[2,128,512]{2,1,0:T(8,128)(2,1)S(1)} %copy-done, pred[128,512]{1,0:T(8,128)(4,1)S(1)} %broadcast_compare_fusion, s32[512]{0:T(512)S(1)} %iota_add_fusion, s32[256]{0:T(256)S(1)} %iota_add_fusion.1), kind=kOutput, calls=%fused_computation.18 | convolution fusion | flops 69402624 | bytes 461824 | tf_op jit(solution)/shard_map/kbp,qp->kbq/dot_general | solution.py:87
  16.2 0.0 copy-start.2
  16.2 0.2 fusion.55
  16.5 0.2 fusion.57
  16.7 0.3 fusion.3
  17.0 0.3 fusion.4
  17.3 0.1 copy.20
  17.4 0.1 broadcast_in_dim.73
  17.5 0.0 copy-start.3
  17.5 1.4 dynamic_update_slice.3
  18.9 1.1 maximum_subtract_fusion
  20.0 0.0 all-gather.5.cloned.1.call-update
  20.0 0.2 all-gather.7.cloned.1.call-start
  20.3 0.7 fusion.104
  23.5 31.9 %all-gather.5.cloned.1.call-done = f32[8,2,256,256]{2,3,0,1:T(8,128)} async-done(((f32[2,2,256,256]{2,3,0,1:T(8,128)}), f32[8,2,256,256]{2,3,0,1:T(8,128)}) %all-gather.5.cloned.1.call-update) | async-done | bytes 4194320 | tf_op jit(solution)/shard_map/all_gather | solution.py:106
  55.4 2.6 %reduce_sum.63 = f32[2,2,256,256]{2,3,0,1:T(8,128)S(1)} reduce(f32[4,2,2,256,256]{3,4,1,0,2:T(8,128)} %bitcast.135, f32[]{:T(128)} %constant.184.clone.1), dimensions={0}, to_apply=%region_0.1 | reduce | flops 786432 | bytes 5242884 | tf_op jit(solution)/shard_map/reduce_sum | solution.py:106
  58.0 0.1 negate_convert_fusion
  58.1 0.2 fusion.43
  58.3 0.2 fusion.44
  58.5 2.2 %fusion.10 = f32[2,128,512]{2,1,0:T(8,128)S(1)} fusion(f32[2,256,128]{2,1,0:T(8,128)S(1)} %fusion.43, bf16[2,2,256,256]{2,3,0,1:T(8,128)(2,1)S(1)} %negate_convert_fusion, s32[512]{0:T(512)S(1)} %iota_add_fusion, s32[256]{0:T(256)S(1)} %iota_add_fusion.1, bf16[256,512]{1,0:T(8,128)(2,1)S(1)} %get-tuple-element.162, s32[]{:T(128)S(6)} %select_n.122), kind=kOutput, calls=%fused_computation.21 | convolution fusion | flops 102891520 | bytes 1117188 | tf_op jit(solution)/shard_map/kns,sp->knp/dot_general | solution.py:68
  60.8 3.1 %fusion.5 = f32[2,128,512]{2,1,0:T(8,128)S(1)} fusion(f32[2,128,512]{2,1,0:T(8,128)S(1)} %fusion.10, f32[2,256,128]{2,1,0:T(8,128)S(1)} %fusion.44, pred[128,512]{1,0:T(8,128)(4,1)S(1)} %broadcast_compare_fusion, bf16[2,2,256,256]{2,3,0,1:T(8,128)(2,1)S(1)} %negate_convert_fusion, s32[512]{0:T(512)S(1)} %iota_add_fusion, s32[256]{0:T(256)S(1)} %iota_add_fusion.1, ...), kind=kOutput, calls=%fused_computation.12 | convolution fusion | flops 103284736 | bytes 1707012 | tf_op jit(solution)/shard_map/kns,sp->knp/dot_general | solution.py:70
  63.9 3.2 %collective-permute-start = (f32[2,33,512]{2,1,0:T(8,128)S(1)}, f32[2,33,512]{2,1,0:T(8,128)S(1)}, u32[]{:S(2)}, u32[]{:S(2)}) collective-permute-start(f32[2,33,512]{2,1,0:T(8,128)S(1)} %pad_maximum_fusion.2), channel_id=1, source_target_pairs={{1,0},{2,1},{3,2},{5,4},{6,5},{7,6},{9,8},{10,9},{11,10},{13,12},{... | collective-permute-start | bytes 405512 | tf_op jit(solution)/shard_map/ppermute | solution.py:15
  67.2 0.0 copy-start.4
  68.6 1.3 collective-permute-done
  70.0 0.2 fusion.21
  70.3 1.0 broadcast_multiply_fusion
  71.3 0.0 all-gather.7.cloned.1.call-update
  71.3 0.6 dynamic-slice
  71.9 0.7 slice_reduce_fusion
  72.6 1.3 dynamic-update-slice
  73.9 1.4 dynamic-update-slice.1
  75.2 10.4 %all-reduce.8 = (s32[8]{0:T(128)S(1)}, s32[8]{0:T(128)S(1)}) all-reduce(s32[8]{0:T(128)S(1)} %dynamic-update-slice, s32[8]{0:T(128)S(1)} %dynamic-update-slice.1), channel_id=1, replica_groups=mesh['tm'=8,'rows'=4] {'tm'}, use_global_device_ids=true, to_apply=%add.6 | all-reduce | flops 16 | bytes 128
  87.0 0.1 slice_convert_fusion.1
  87.1 0.1 slice.142
  87.3 0.1 slice.146
  87.4 0.1 slice_bitcast_fusion
  87.5 39.8 %all-gather.7.cloned.1.call-done = f32[1280,512]{1,0:T(8,128)} async-done(((f32[160,512]{1,0:T(8,128)}), f32[1280,512]{1,0:T(8,128)}) %all-gather.7.cloned.1.call-update) | async-done | bytes 2621456 | tf_op jit(solution)/shard_map/all_gather | solution.py:22
  127.3 18.6 %while.16 = (s32[]{:T(128)}, f32[160,512]{1,0:T(8,128)S(1)}, s32[]{:T(128)}, f32[8,160,512]{2,1,0:T(8,128)}, s32[8]{0:T(128)S(1)}, /*index=5*/s32[8]{0:T(128)S(1...) while((s32[]{:T(128)}, f32[160,512]{1,0:T(8,128)S(1)}, ...), condition=%wide.region_4.6_spmd, body=%wide.region_3.5_spmd.sunk | while | flops 246299 | bytes 1639884 | solution.py:31
  127.3 0.6 dynamic_slice.173
  128.5 0.6 dynamic_slice.174
  129.8 1.2 fusion.110
  131.0 0.6 dynamic_slice.173
  132.3 0.6 dynamic_slice.174
  133.5 1.2 fusion.110
  134.7 0.6 dynamic_slice.173
  136.0 0.6 dynamic_slice.174
  137.2 1.2 fusion.110
  138.5 0.6 dynamic_slice.173
  139.7 0.6 dynamic_slice.174
  140.9 1.2 fusion.110
  142.2 0.6 dynamic_slice.173
  143.5 0.6 dynamic_slice.174
  144.7 1.2 fusion.110
  146.0 0.1 pad_dynamic-slice_fusion.11
  146.1 1.1 fusion.38
  147.2 2.6 %maximum_add_fusion = f32[2]{0:T(128)S(1)} fusion(f32[1]{0:T(128)} %bitcast.38, f32[1]{0:T(128)} %bitcast.37, f32[1]{0:T(128)} %bitcast.44, f32[1]{0:T(128)} %bitcast.43), kind=kLoop, calls=%fused_computation.140 | loop fusion | flops 6 | bytes 24 | tf_op jit(solution)/shard_map/add | solution.py:160
  149.8 46.4 %psum.7 = f32[2]{0:T(128)S(1)} all-reduce(f32[2]{0:T(128)S(1)} %maximum_add_fusion), channel_id=1, replica_groups=mesh['tm'=8,'rows'=4] {'tm','rows'}, use_global_device_ids=true, to_apply=%region_9.11 | all-reduce | flops 2 | bytes 16 | tf_op jit(solution)/shard_map/psum | solution.py:163
  196.2 0.5 negate_multiply_fusion
  196.8 0.8 pad_maximum_fusion
  (31 shorter events, 0.4 us)
Async XLA Ops:
  7.2 6.8 %copy-start = (bf16[2,128,512]{2,1,0:T(8,128)(2,1)S(1)}, bf16[2,128,512]{2,1,0:T(8,128)(2,1)}, u32[]{:S(2)}) copy-start(bf16[2,128,512]{2,1,0:T(8,128)(2,1)} %param.8) | copy-start | bytes 786436
  7.2 48.2 %all-gather.5.cloned.1.call-start = ((), (), s32[]{:S(2)}) async-start(), calls=%async_computation | async-start | bytes 5242880 | tf_op jit(solution)/shard_map/all_gather | solution.py:106
  10.7 47.8 %copy-start.1 = (bf16[256,512]{1,0:T(8,128)(2,1)}, bf16[256,512]{1,0:T(8,128)(2,1)S(1)}, u32[]{:S(2)}) copy-start(bf16[256,512]{1,0:T(8,128)(2,1)S(1)} %get-tuple-element.162) | copy-start | bytes 786436
  16.2 1.1 copy-start.2
  17.5 2.8 %copy-start.3 = (s32[2,2]{1,0:T(2,128)S(1)}, s32[2,2]{1,0:T(2,128)}, u32[]{:S(2)}) copy-start(s32[2,2]{1,0:T(2,128)} %param.10) | copy-start | bytes 52
  20.0 107.2 %all-gather.7.cloned.1.call-start = ((), (), s32[]{:S(2)}) async-start(), calls=%async_computation.1 | async-start | bytes 2949120 | tf_op jit(solution)/shard_map/all_gather | solution.py:22
  63.9 6.1 %collective-permute-start = (f32[2,33,512]{2,1,0:T(8,128)S(1)}, f32[2,33,512]{2,1,0:T(8,128)S(1)}, u32[]{:S(2)}, u32[]{:S(2)}) collective-permute-start(f32[2,33,512]{2,1,0:T(8,128)S(1)} %pad_maximum_fusion.2), channel_id=1, source_target_pairs={{1,0},{2,1},{3,2},{5,4},{6,5},{7,6},{9,8},{10,9},{11,10},{13,12},{... | collective-permute-start | bytes 405512 | tf_op jit(solution)/shard_map/ppermute | solution.py:15
  67.2 4.1 %copy-start.4 = (u32[32]{0:T(128)S(1)}, u32[32]{0:T(128)}, u32[]{:S(2)}) copy-start(u32[32]{0:T(128)} %constant.215) | copy-start | bytes 388
Sparse Core Ops, SparseCore 0:
  20.1 35.1 all-gather.4
  71.4 55.8 all-gather.6
